TPU v7x, 512 devices: a whole 4x4x16 slice. The times are simulated.
512 devices in a mesh: row: 32 (over z, core), col: 16 (over x, y).
Axes of the slice: x: 4, y: 4, z: 16, core: 2. Of those that a mesh axis runs over, the one named last changes fastest.
Arguments:
- front_entries: float32 [16384, 16384], P('row', 'col'), may hold values from 0 to 3, as said below
- tile_group: int32 [32], replicated, may hold values from 0 to 3
- child_factor: bfloat16 [16384, 256], P('row', 'col'), may hold values from -0.375 to 0.375
- row_map: int32 [128], replicated, may hold values from 0 to 127, as said below
Outputs:
- factor_panels: bfloat16 [16384, 512], P('row', 'col')
- schur_block: float32 [16384, 16384], P('row', 'col')
Inputs may be any that keep to these rules, and one draw needn't show every extreme that they name: `front_entries`: Symmetric; assembled is positive definite. `row_map`: A permutation of the parent tiles. The tile in row block r (blocks of 512 rows) goes to a parent tile in row block r or in the row block whose index differs from r in the highest bit.
All inputs are finite; a program needn't handle non-finite values.
Results may differ from a plain program's by a relative error of at most 0.0026.
Values may be sent and summed in bfloat16 or wider, within the bound.
A program may use at most 64 MiB of HBM per device.

v0:
```python
import jax
import jax.numpy as jnp
from jax import lax
from jax.sharding import PartitionSpec as P

PW = 256
NP = 2
TS = 128
MT = 512


def swapped(value, axis, stride):
    mask = 2**stride
    pairs = [(source, source ^ mask) for source in range(lax.axis_size(axis))]
    return lax.ppermute(value, axis, pairs)


def broadcast(value, axis, source):
    kept = jnp.where(lax.axis_index(axis) == source, value, 0).astype(value.dtype)
    return lax.psum(kept, axis)


def panel_columns(matrix, offset, width_cols, fan_ratio, block_rows):
    return jnp.concatenate(
        [
            matrix[:, q * block_rows + offset : q * block_rows + offset + width_cols]
            for q in range(fan_ratio)
        ],
        axis=1,
    )


def outer_rows(left, right):
    return jnp.einsum("ik,jk->ij", left, right, preferred_element_type=jnp.float32)


def subtract_block(matrix, lead_rows, owner, low, col_from, col_to, base_col):
    region = matrix[low:, base_col + col_from : base_col + col_to]
    return matrix.at[low:, base_col + col_from : base_col + col_to].set(
        region - outer_rows(lead_rows, owner[col_from:col_to])
    )


def right_solve(lower_factor, strip):
    return lax.linalg.triangular_solve(
        lower_factor, strip, left_side=False, lower=True, transpose_a=True
    )


def local(front_entries, tile_group, child_factor, row_map):
    row_count = lax.axis_size("row")
    col_count = lax.axis_size("col")
    fan_ratio = row_count // col_count
    local_rows = front_entries.shape[0]
    local_cols = front_entries.shape[1]
    my_row = lax.axis_index("row")
    my_col = lax.axis_index("col")
    row_tiles = local_rows // MT
    col_tiles = local_cols // MT
    group_rows = lax.dynamic_slice_in_dim(tile_group, my_row * row_tiles, row_tiles)
    group_cols = lax.dynamic_slice_in_dim(tile_group, my_col * col_tiles, col_tiles)
    same_group = (group_rows[:, None] == group_cols[None, :]).astype(jnp.float32)
    masked = (
        front_entries.reshape(row_tiles, MT, col_tiles, MT) * same_group[:, None, :, None]
    ).reshape(local_rows, local_cols)
    child_full = lax.all_gather(child_factor, "col", axis=1, tiled=True)
    child_width = child_full.shape[1]
    partner_full = swapped(child_full, "row", row_count.bit_length() - 2)
    tile_count = local_rows // TS
    partner_row = jnp.bitwise_xor(my_row, row_count // 2)
    own_map = lax.dynamic_slice_in_dim(row_map, my_row * tile_count, tile_count)
    partner_map = lax.dynamic_slice_in_dim(row_map, partner_row * tile_count, tile_count)
    slot_ids = my_row * tile_count + jnp.arange(tile_count, dtype=jnp.int32)

    def place_tiles(tile_map, source):
        chooser = (tile_map[None, :] == slot_ids[:, None]).astype(jnp.bfloat16)
        placed = jnp.dot(
            chooser,
            source.reshape(tile_count, TS * child_width),
            preferred_element_type=jnp.float32,
        )
        return placed.astype(jnp.bfloat16).reshape(local_rows, child_width)

    own_parent = place_tiles(own_map, child_full)
    partner_parent = place_tiles(partner_map, partner_full)
    lower_half = my_row < row_count // 2
    child_wide = jnp.where(
        lower_half,
        jnp.concatenate([own_parent, partner_parent], axis=1),
        jnp.concatenate([partner_parent, own_parent], axis=1),
    )
    child_owners = [broadcast(child_wide, "row", fan_ratio * my_col + q) for q in range(fan_ratio)]
    matrix = jnp.concatenate(
        [
            masked[:, q * local_rows : (q + 1) * local_rows]
            + outer_rows(child_wide, child_owners[q])
            for q in range(fan_ratio)
        ],
        axis=1,
    )
    row_share = PW // row_count
    col_share = PW // col_count
    local_ids = jnp.arange(local_rows)
    coming = None
    outputs = []
    for k in range(NP):
        offset = k * row_share
        panel_strip = panel_columns(matrix, offset, row_share, fan_ratio, local_rows)
        corner = panel_strip[offset : offset + row_share]
        gathered = lax.all_gather(corner, ("row", "col"), axis=0, tiled=True)
        diagonal = (
            gathered.reshape(row_count, col_count, row_share, col_share)
            .transpose(0, 2, 1, 3)
            .reshape(PW, PW)
        )
        lower_factor = jnp.linalg.cholesky(diagonal)
        whole_strip = lax.all_gather(panel_strip, "col", axis=1, tiled=True)
        rounded = right_solve(lower_factor, whole_strip).astype(jnp.bfloat16)
        own_lower = lax.dynamic_slice_in_dim(lower_factor, my_row * row_share, row_share).astype(
            jnp.bfloat16
        )
        rounded = jnp.where((local_ids < offset)[:, None], jnp.zeros_like(rounded), rounded)
        rounded = rounded.at[offset : offset + row_share].set(own_lower)
        outputs.append(lax.dynamic_slice_in_dim(rounded, my_col * col_share, col_share, 1))
        owners = [broadcast(rounded, "row", fan_ratio * my_col + q) for q in range(fan_ratio)]
        low = offset + row_share
        lead_rows = rounded[low:]
        for q in range(fan_ratio):
            matrix = subtract_block(
                matrix, lead_rows, owners[q], low, low, local_rows, q * local_rows
            )
    pivot_done = NP * row_share
    row_keep = local_ids >= pivot_done
    col_keep = jnp.arange(local_cols) % local_rows >= pivot_done
    schur_block = jnp.where(row_keep[:, None] & col_keep[None, :], matrix, jnp.zeros_like(matrix))
    factor_panels = jnp.concatenate(outputs, axis=1)
    return (factor_panels, schur_block)


def solution(mesh):
    placed = (P("row", "col"), P(), P("row", "col"), P())
    return jax.shard_map(
        local,
        mesh=mesh,
        in_specs=placed,
        out_specs=(P("row", "col"), P("row", "col")),
        check_vma=False,
    )
```

profile of v0, /device:TPU:1, one launch (start us, length us, event | category | flops | bytes accessed | tf_op | source)
XLA Modules:
  0.0 1302.7 jit_solution(17513636110733798873)
XLA Ops:
  7.2 19.7 %all_gather.15 = bf16[512,256]{0,1:T(8,128)(2,1)S(1)} all-gather(bf16[512,16]{0,1:T(8,128)(2,1)} %param.21), channel_id=1, replica_groups=mesh['row'=32,'col'=16] {'col'}, dimensions={1}, use_global_device_ids=true | all-gather | bytes 278528 | tf_op jit(solution)/shard_map/all_gather | solution.py:66
  26.9 15.4 %collective-permute-start = (bf16[512,256]{0,1:T(8,128)(2,1)S(1)}, bf16[512,256]{0,1:T(8,128)(2,1)S(1)}, u32[]{:S(2)}, u32[]{:S(2)}) collective-permute-start(bf16[512,256]{0,1:T(8,128)(2,1)S(1)} %all_gather.15), channel_id=1, source_target_pairs={{0,256},{16,272},{32,288},{48,304},{64,320},{80,336},{96,352},{112... | collective-permute-start | bytes 786440 | tf_op jit(solution)/shard_map/ppermute | solution.py:15
  42.7 0.8 fusion.44
  44.1 0.6 dynamic_slice.24
  44.7 0.7 compare_convert_fusion
  45.5 1.9 copy.30
  48.3 1.3 broadcast_select_fusion.1
  49.6 1.5 broadcast_multiply_fusion
  51.2 226.5 %all-reduce.12.cloned.1.call-done = (bf16[512,512]{1,0:T(8,128)(2,1)}, bf16[512,512]{1,0:T(8,128)(2,1)}) async-done(((bf16[512,512]{1,0:T(8,128)(2,1)}, bf16[512,512]{1,0:T(8,128)(2,1)}), (bf16[512,512]{1,0:T(8,128)(2,1)}, bf16[512,512]{1,0:T(8,128)(2,1)})) %all-reduce.12.cloned.1.call-update) | async-done | bytes 1048592 | tf_op jit(solution)/shard_map/psum | solution.py:20
  277.7 2.1 convolution_add_fusion.1
  279.8 0.5 convolution_add_fusion
  280.3 1.0 copy-done.1
  281.4 198.2 %all_gather.16 = f32[4096,16]{1,0:T(8,128)S(1)} all-gather(f32[8,16]{1,0:T(8,128)S(1)} %copy.33), channel_id=1, replica_groups=mesh['row'=32,'col'=16] {'row','col'}, dimensions={0}, use_global_device_ids=true | all-gather | bytes 262656 | tf_op jit(solution)/shard_map/all_gather | solution.py:110
  479.9 0.9 reshape.255
  481.1 11.7 cholesky.130
  492.8 9.8 custom-call.13
  503.1 11.9 cholesky.147
  515.0 0.6 compare_reduce_fusion.2
  515.7 0.6 compare_reduce_fusion.3
  517.6 3.8 while.10
  517.7 0.6 fusion.59
  518.2 1.3 bitcast_dynamic-update-slice_fusion.4
  519.6 0.6 fusion.59
  520.2 1.3 bitcast_dynamic-update-slice_fusion.4
  521.5 19.7 %custom-call.14 = f32[2,128,128]{1,2,0:T(8,128)S(1)} custom-call(f32[2,128,128]{2,1,0:T(8,128)S(1)} %get-tuple-element.90), custom_call_target="InvertDiagBlocksLowerTriangular" | custom-call | tf_op jit(solution)/shard_map/triangular_solve/custom-call.0 | solution.py:45
  541.2 16.2 %all_gather.17 = f32[512,256]{0,1:T(8,128)S(1)} all-gather(f32[512,16]{0,1:T(8,128)S(1)} %pad_maximum_fusion.1), channel_id=1, replica_groups=mesh['row'=32,'col'=16] {'col'}, dimensions={1}, use_global_device_ids=true | all-gather | bytes 557056 | tf_op jit(solution)/shard_map/all_gather | solution.py:117
  557.4 0.4 fusion.7
  557.8 0.4 convolution_subtract_fusion.5
  558.2 0.4 fusion.22
  559.1 0.8 broadcast_select_fusion.3
  560.0 1.4 pad_maximum_fusion
  561.5 209.2 %all-reduce.10.cloned.1.call-done = (bf16[512,256]{0,1:T(8,128)(2,1)}, bf16[512,256]{0,1:T(8,128)(2,1)}) async-done(((bf16[512,256]{0,1:T(8,128)(2,1)}, bf16[512,256]{0,1:T(8,128)(2,1)}), (bf16[512,256]{0,1:T(8,128)(2,1)}, bf16[512,256]{0,1:T(8,128)(2,1)})) %all-reduce.10.cloned.1.call-update) | async-done | bytes 524304 | tf_op jit(solution)/shard_map/psum | solution.py:20
  770.6 2.6 convolution_subtract_fusion.1
  773.2 5.4 scatter.21
  778.6 1.6 convolution_subtract_fusion
  780.2 3.4 scatter.24
  783.8 197.6 %all_gather.18 = f32[4096,16]{1,0:T(8,128)S(1)} all-gather(f32[8,16]{1,0:T(8,128)S(1)} %copy.38), channel_id=1, replica_groups=mesh['row'=32,'col'=16] {'row','col'}, dimensions={0}, use_global_device_ids=true | all-gather | bytes 262656 | tf_op jit(solution)/shard_map/all_gather | solution.py:110
  981.5 1.7 copy.39
  983.2 2.6 reshape.257
  986.0 11.7 cholesky.164
  997.8 9.8 custom-call.15
  1008.1 11.7 cholesky.181
  1019.8 0.6 compare_reduce_fusion
  1020.5 0.6 compare_reduce_fusion.1
  1022.4 4.0 while.11
  1022.5 0.6 fusion.60
  1023.1 1.4 bitcast_dynamic-update-slice_fusion.5
  1024.5 0.6 fusion.60
  1025.1 1.4 bitcast_dynamic-update-slice_fusion.5
  1026.5 19.9 %custom-call.16 = f32[2,128,128]{1,2,0:T(8,128)S(1)} custom-call(f32[2,128,128]{2,1,0:T(8,128)S(1)} %get-tuple-element.91), custom_call_target="InvertDiagBlocksLowerTriangular" | custom-call | tf_op jit(solution)/shard_map/triangular_solve/custom-call.0 | solution.py:45
  1046.4 16.3 %all_gather.19 = f32[512,256]{0,1:T(8,128)S(1)} all-gather(f32[512,16]{0,1:T(8,128)S(1)} %pad_maximum_fusion.2), channel_id=1, replica_groups=mesh['row'=32,'col'=16] {'col'}, dimensions={1}, use_global_device_ids=true | all-gather | bytes 557056 | tf_op jit(solution)/shard_map/all_gather | solution.py:117
  1062.6 0.4 fusion.3
  1063.1 0.4 convolution_subtract_fusion.4
  1063.5 0.4 fusion.18
  1064.1 0.6 scatter.25
  1064.7 0.8 broadcast_select_fusion.2
  1065.6 0.6 pad_maximum_fusion.3
  1066.2 210.0 %all-reduce.8.cloned.1.call-done = (bf16[512,256]{0,1:T(8,128)(2,1)}, bf16[512,256]{0,1:T(8,128)(2,1)}) async-done(((bf16[512,256]{0,1:T(8,128)(2,1)}, bf16[512,256]{0,1:T(8,128)(2,1)}), (bf16[512,256]{0,1:T(8,128)(2,1)}, bf16[512,256]{0,1:T(8,128)(2,1)})) %all-reduce.8.cloned.1.call-update) | async-done | bytes 524304 | tf_op jit(solution)/shard_map/psum | solution.py:20
  1276.2 2.6 convolution_subtract_fusion.3
  1278.8 5.4 scatter.26
  1284.2 1.6 convolution_subtract_fusion.2
  1285.8 5.6 scatter.29
  1291.4 1.6 and_select_fusion
  1293.0 2.9 copy.45
  (78 shorter events, 4.9 us)
Async XLA Ops:
  7.2 36.9 %copy-start.5 = (s32[32]{0:T(128)S(1)}, s32[32]{0:T(128)}, u32[]{:S(2)}) copy-start(s32[32]{0:T(128)} %param.20) | copy-start | bytes 388
  7.2 270.5 %all-reduce.12.cloned.1.call-start = ((), (), s32[]{:S(2)}) async-start(), calls=%async_computation.2 | async-start | bytes 2097152 | tf_op jit(solution)/shard_map/psum | solution.py:20
  26.9 20.5 %collective-permute-start = (bf16[512,256]{0,1:T(8,128)(2,1)S(1)}, bf16[512,256]{0,1:T(8,128)(2,1)S(1)}, u32[]{:S(2)}, u32[]{:S(2)}) collective-permute-start(bf16[512,256]{0,1:T(8,128)(2,1)S(1)} %all_gather.15), channel_id=1, source_target_pairs={{0,256},{16,272},{32,288},{48,304},{64,320},{80,336},{96,352},{112... | collective-permute-start | bytes 786440 | tf_op jit(solution)/shard_map/ppermute | solution.py:15
  48.3 2.9 copy-start.2
  49.6 721.1 %all-reduce.10.cloned.1.call-start = ((), (), s32[]{:S(2)}) async-start(), calls=%async_computation.1 | async-start | bytes 1048576 | tf_op jit(solution)/shard_map/psum | solution.py:20
  51.2 228.6 %copy-start = (f32[512,1024]{0,1:T(8,128)S(1)}, f32[512,1024]{0,1:T(8,128)}, u32[]{:S(2)}) copy-start(f32[512,1024]{0,1:T(8,128)} %broadcast_multiply_fusion) | copy-start | bytes 6291460
  277.7 2.1 copy-start.3
  277.7 2.1 copy-start.6
  280.3 1.0 copy-start.1
  560.0 716.2 %all-reduce.8.cloned.1.call-start = ((), (), s32[]{:S(2)}) async-start(), calls=%async_computation | async-start | bytes 1048576 | tf_op jit(solution)/shard_map/psum | solution.py:20
  1276.2 8.0 copy-start.4
Sparse Core Ops, SparseCore 0:
  49.7 227.9 all-reduce.11
  560.1 210.4 all-reduce.9
  1065.7 210.4 all-reduce.7
where the time goes:
time: 1310 us; the launch traced here: 1300 us
  waiting for transfers between devices  646 us (49%)
  blocking collectives  448 us (34%)
  other arithmetic  119 us (9%)
  local copies, waits for them, and re-layouts  42.4 us (3%)
  between operations  17.1 us (1%)
  starting transfers between devices  15.5 us (1%)
  matrix products  15 us (1%)
    psum x3, waiting for transfers between devices, broadcast(): return lax.psum(kept, axis)  646 us
    all_gather x2, blocking collectives, local(): gathered = lax.all_gather(corner, ('row', 'col'), axis=0, tiled=True)  396 us
    another operation x14, other arithmetic, local(): lower_factor = jnp.linalg.cholesky(diagonal)  69.3 us
    another operation x5, other arithmetic, right_solve(): lax.linalg.triangular_solve(lower_factor, strip, left_side=False, lower=T...  39.7 us
    all_gather x2, blocking collectives, local(): whole_strip = lax.all_gather(panel_strip, 'col', axis=1, tiled=True)  32.5 us
  transfers between devices with their start and end apart: 4, of which 3 were waited for; matrix products, arithmetic and copies ran while one was open for 1% of the time, Pallas kernels for 0%

commit v1 on v0

--- a/solution.py
+++ b/solution.py
@@ -17,7 +17,7 @@
 
 def broadcast(value, axis, source):
     kept = jnp.where(lax.axis_index(axis) == source, value, 0).astype(value.dtype)
-    return lax.psum(kept, axis)
+    return jnp.sum(lax.all_gather(kept, axis), axis=0)
 
 
 def panel_columns(matrix, offset, width_cols, fan_ratio, block_rows):

time: 1310 us -> 1250 us (0.954)
  waiting for transfers between devices: 646 us -> 485 us
  other arithmetic: 119 us -> 168 us
  local copies, waits for them, and re-layouts: 42.4 us -> 83.8 us
    psum x3 -> x0, waiting for transfers between devices: 646 us -> none  [broadcast(): return lax.psum(kept, axis)]
    all_gather x0 -> x6, waiting for transfers between devices: none -> 481 us  [broadcast(): return jnp.sum(lax.all_gather(kept, axis), axis=0)]
    reduce_sum x0 -> x6, other arithmetic: none -> 48.5 us  [broadcast(): return jnp.sum(lax.all_gather(kept, axis), axis=0)]
    unnamed x18 -> x20, local copies, waits for them, and re-layouts: 5.87 us -> 48.1 us
  transfers between devices with their start and end apart: 4 -> 7, of which waited for: 3 -> 7; matrix products, arithmetic and copies ran while one was open for 1% -> 5% of each run, Pallas kernels for 0% -> 0%
where the time goes in v1:
time: 1250 us; the launch traced here: 1240 us
  waiting for transfers between devices  485 us (39%)
  blocking collectives  457 us (37%)
  other arithmetic  168 us (13%)
  local copies, waits for them, and re-layouts  83.8 us (7%)
  between operations  17.4 us (1%)
  starting transfers between devices  15.8 us (1%)
  matrix products  14.6 us (1%)
    all_gather x6, waiting for transfers between devices, broadcast(): return jnp.sum(lax.all_gather(kept, axis), axis=0)  481 us
    all_gather x2, blocking collectives, local(): gathered = lax.all_gather(corner, ('row', 'col'), axis=0, tiled=True)  400 us
    another operation x14, other arithmetic, local(): lower_factor = jnp.linalg.cholesky(diagonal)  69.6 us
    reduce_sum x6, other arithmetic, broadcast(): return jnp.sum(lax.all_gather(kept, axis), axis=0)  48.5 us
    unnamed x20, local copies, waits for them, and re-layouts  48.1 us
    another operation x5, other arithmetic, right_solve(): lax.linalg.triangular_solve(lower_factor, strip, left_side=False, lower=T...  39.4 us
    all_gather x2, blocking collectives, local(): whole_strip = lax.all_gather(panel_strip, 'col', axis=1, tiled=True)  37.6 us
  transfers between devices with their start and end apart: 7, of which 7 were waited for; matrix products, arithmetic and copies ran while one was open for 5% of the time, Pallas kernels for 0%

profile of v1, /device:TPU:1, one launch (start us, length us, event | category | flops | bytes accessed | tf_op | source)
XLA Modules:
  0.0 1241.3 jit_solution(6707079014376973267)
XLA Ops:
  7.2 19.7 %all_gather.47 = bf16[512,256]{0,1:T(8,128)(2,1)S(1)} all-gather(bf16[512,16]{0,1:T(8,128)(2,1)} %param.21), channel_id=1, replica_groups=mesh['row'=32,'col'=16] {'col'}, dimensions={1}, use_global_device_ids=true | all-gather | bytes 278528 | tf_op jit(solution)/shard_map/all_gather | solution.py:66
  26.9 15.4 %collective-permute-start = (bf16[512,256]{0,1:T(8,128)(2,1)S(1)}, bf16[512,256]{0,1:T(8,128)(2,1)S(1)}, u32[]{:S(2)}, u32[]{:S(2)}) collective-permute-start(bf16[512,256]{0,1:T(8,128)(2,1)S(1)} %all_gather.47), channel_id=1, source_target_pairs={{0,256},{16,272},{32,288},{48,304},{64,320},{80,336},{96,352},{112... | collective-permute-start | bytes 786440 | tf_op jit(solution)/shard_map/ppermute | solution.py:15
  42.3 0.8 fusion.46
  44.0 2.3 collective-permute-done
  47.3 1.2 broadcast_select_fusion.1
  48.5 0.7 all-gather.13.cloned.1.call-update
  50.1 0.7 compare_convert_fusion
  50.9 1.9 copy.30
  52.8 1.5 broadcast_multiply_fusion
  54.3 0.9 reshape.350
  55.2 118.6 %all-gather.11.cloned.1.call-done = bf16[32,512,512]{2,1,0:T(8,128)(2,1)} async-done(((bf16[1,512,512]{2,1,0:T(8,128)(2,1)}), bf16[32,512,512]{2,1,0:T(8,128)(2,1)}) %all-gather.11.cloned.1.call-update) | async-done | bytes 16777232 | tf_op jit(solution)/shard_map/all_gather | solution.py:20
  173.8 9.6 reduce_sum.72
  183.4 1.7 convolution_add_fusion.1
  185.1 95.5 %all-gather.13.cloned.1.call-done = bf16[32,512,512]{2,1,0:T(8,128)(2,1)} async-done(((bf16[1,512,512]{2,1,0:T(8,128)(2,1)}), bf16[32,512,512]{2,1,0:T(8,128)(2,1)}) %all-gather.13.cloned.1.call-update) | async-done | bytes 16777232 | tf_op jit(solution)/shard_map/all_gather | solution.py:20
  280.6 9.6 reduce_sum.73
  290.2 1.7 convolution_add_fusion
  291.9 0.9 copy-done.3
  292.9 18.8 %all_gather.51 = f32[512,256]{0,1:T(8,128)S(1)} all-gather(f32[512,16]{0,1:T(8,128)S(1)} %pad_maximum_fusion.1), channel_id=1, replica_groups=mesh['row'=32,'col'=16] {'col'}, dimensions={1}, use_global_device_ids=true | all-gather | bytes 557056 | tf_op jit(solution)/shard_map/all_gather | solution.py:117
  311.7 199.9 %all_gather.50 = f32[4096,16]{1,0:T(8,128)S(1)} all-gather(f32[8,16]{1,0:T(8,128)S(1)} %copy.33), channel_id=1, replica_groups=mesh['row'=32,'col'=16] {'row','col'}, dimensions={0}, use_global_device_ids=true | all-gather | bytes 262656 | tf_op jit(solution)/shard_map/all_gather | solution.py:110
  512.0 0.9 reshape.352
  513.1 11.7 cholesky.130
  525.5 9.8 custom-call.13
  535.8 12.1 cholesky.147
  550.1 4.0 while.10
  550.7 1.4 bitcast_dynamic-update-slice_fusion.4
  552.7 1.4 bitcast_dynamic-update-slice_fusion.4
  554.0 19.7 %custom-call.14 = f32[2,128,128]{1,2,0:T(8,128)S(1)} custom-call(f32[2,128,128]{2,1,0:T(8,128)S(1)} %get-tuple-element.90), custom_call_target="InvertDiagBlocksLowerTriangular" | custom-call | tf_op jit(solution)/shard_map/triangular_solve/custom-call.0 | solution.py:45
  575.5 0.8 broadcast_select_fusion.3
  577.0 1.7 pad_maximum_fusion
  578.7 73.2 %all-gather.17.cloned.1.call-done = bf16[16384,256]{0,1:T(8,128)(2,1)} async-done(((bf16[512,256]{0,1:T(8,128)(2,1)}), bf16[16384,256]{0,1:T(8,128)(2,1)}) %all-gather.17.cloned.1.call-update) | async-done | bytes 8388624 | tf_op jit(solution)/shard_map/all_gather | solution.py:20
  651.9 10.4 copy.52
  662.3 7.0 bitcast_reduce_fusion.2
  669.3 60.7 %all-gather.15.cloned.1.call-done = bf16[16384,256]{0,1:T(8,128)(2,1)} async-done(((bf16[512,256]{0,1:T(8,128)(2,1)}), bf16[16384,256]{0,1:T(8,128)(2,1)}) %all-gather.15.cloned.1.call-update) | async-done | bytes 8388624 | tf_op jit(solution)/shard_map/all_gather | solution.py:20
  730.1 10.4 copy.51
  740.5 7.3 bitcast_reduce_fusion.3
  747.8 1.6 convolution_subtract_fusion.1
  749.4 5.4 scatter.21
  754.8 1.6 convolution_subtract_fusion
  756.4 5.6 scatter.24
  762.2 18.8 %all_gather.57 = f32[512,256]{0,1:T(8,128)S(1)} all-gather(f32[512,16]{0,1:T(8,128)S(1)} %pad_maximum_fusion.2), channel_id=1, replica_groups=mesh['row'=32,'col'=16] {'col'}, dimensions={1}, use_global_device_ids=true | all-gather | bytes 557056 | tf_op jit(solution)/shard_map/all_gather | solution.py:117
  781.0 199.7 %all_gather.56 = f32[4096,16]{1,0:T(8,128)S(1)} all-gather(f32[8,16]{1,0:T(8,128)S(1)} %copy.38), channel_id=1, replica_groups=mesh['row'=32,'col'=16] {'row','col'}, dimensions={0}, use_global_device_ids=true | all-gather | bytes 262656 | tf_op jit(solution)/shard_map/all_gather | solution.py:110
  980.7 1.7 copy.39
  982.4 2.8 reshape.354
  986.2 11.7 cholesky.164
  998.5 9.8 custom-call.15
  1008.4 1.0 constant_dynamic-update-slice_fusion
  1009.4 1.1 convolution_subtract_fusion.6
  1010.5 11.7 cholesky.181
  1024.2 3.8 while.11
  1024.8 1.3 bitcast_dynamic-update-slice_fusion.5
  1026.8 1.3 bitcast_dynamic-update-slice_fusion.5
  1028.1 19.7 %custom-call.16 = f32[2,128,128]{1,2,0:T(8,128)S(1)} custom-call(f32[2,128,128]{2,1,0:T(8,128)S(1)} %get-tuple-element.91), custom_call_target="InvertDiagBlocksLowerTriangular" | custom-call | tf_op jit(solution)/shard_map/triangular_solve/custom-call.0 | solution.py:45
  1049.8 0.9 broadcast_select_fusion.2
  1051.9 73.0 %all-gather.21.cloned.1.call-done = bf16[16384,256]{0,1:T(8,128)(2,1)} async-done(((bf16[512,256]{0,1:T(8,128)(2,1)}), bf16[16384,256]{0,1:T(8,128)(2,1)}) %all-gather.21.cloned.1.call-update) | async-done | bytes 8388624 | tf_op jit(solution)/shard_map/all_gather | solution.py:20
  1124.9 10.4 copy.54
  1135.3 7.7 bitcast_reduce_fusion
  1143.0 60.0 %all-gather.19.cloned.1.call-done = bf16[16384,256]{0,1:T(8,128)(2,1)} async-done(((bf16[512,256]{0,1:T(8,128)(2,1)}), bf16[16384,256]{0,1:T(8,128)(2,1)}) %all-gather.19.cloned.1.call-update) | async-done | bytes 8388624 | tf_op jit(solution)/shard_map/all_gather | solution.py:20
  1203.1 10.4 copy.53
  1213.5 7.2 bitcast_reduce_fusion.1
  1221.4 3.3 scatter.26
  1224.7 1.6 convolution_subtract_fusion.2
  1226.3 3.5 scatter.29
  1229.8 1.6 and_select_fusion
  1231.4 2.9 copy.45
  (97 shorter events, 16.3 us)
Async XLA Ops:
  7.2 166.6 %all-gather.11.cloned.1.call-start = ((), (), s32[]{:S(2)}) async-start(), calls=%async_computation | async-start | bytes 17301504 | tf_op jit(solution)/shard_map/all_gather | solution.py:20
  26.9 19.5 %collective-permute-start = (bf16[512,256]{0,1:T(8,128)(2,1)S(1)}, bf16[512,256]{0,1:T(8,128)(2,1)S(1)}, u32[]{:S(2)}, u32[]{:S(2)}) collective-permute-start(bf16[512,256]{0,1:T(8,128)(2,1)S(1)} %all_gather.47), channel_id=1, source_target_pairs={{0,256},{16,272},{32,288},{48,304},{64,320},{80,336},{96,352},{112... | collective-permute-start | bytes 786440 | tf_op jit(solution)/shard_map/ppermute | solution.py:15
  46.7 2.8 copy-start.5
  48.5 232.1 %all-gather.13.cloned.1.call-start = ((), (), s32[]{:S(2)}) async-start(), calls=%async_computation.1 | async-start | bytes 17301504 | tf_op jit(solution)/shard_map/all_gather | solution.py:20
  49.2 602.7 %all-gather.17.cloned.1.call-start = ((), (), s32[]{:S(2)}) async-start(), calls=%async_computation.3 | async-start | bytes 8650752 | tf_op jit(solution)/shard_map/all_gather | solution.py:20
  55.2 128.2 %copy-start.2 = (f32[512,1024]{0,1:T(8,128)S(1)}, f32[512,1024]{0,1:T(8,128)}, u32[]{:S(2)}) copy-start(f32[512,1024]{0,1:T(8,128)} %broadcast_multiply_fusion) | copy-start | bytes 6291460
  185.1 106.8 %copy-start = (f32[512,512]{0,1:T(8,128)}, f32[512,512]{0,1:T(8,128)S(1)}, u32[]{:S(2)}) copy-start(f32[512,512]{0,1:T(8,128)S(1)} %convolution_add_fusion.1) | copy-start | bytes 3145732
  291.8 1.0 copy-start.3
  576.3 153.8 %all-gather.15.cloned.1.call-start = ((), (), s32[]{:S(2)}) async-start(), calls=%async_computation.2 | async-start | bytes 8650752 | tf_op jit(solution)/shard_map/all_gather | solution.py:20
  576.9 548.0 %all-gather.21.cloned.1.call-start = ((), (), s32[]{:S(2)}) async-start(), calls=%async_computation.5 | async-start | bytes 8650752 | tf_op jit(solution)/shard_map/all_gather | solution.py:20
  740.5 7.3 copy-start.1
  985.4 0.7 copy-start.4
  1050.6 152.4 %all-gather.19.cloned.1.call-start = ((), (), s32[]{:S(2)}) async-start(), calls=%async_computation.4 | async-start | bytes 8650752 | tf_op jit(solution)/shard_map/all_gather | solution.py:20
Sparse Core Ops, SparseCore 0:
  48.6 125.1 all-gather.10
  175.9 104.6 all-gather.12
  576.4 75.4 all-gather.16
  653.9 76.1 all-gather.14
  1050.8 74.0 all-gather.20
  1126.9 76.1 all-gather.18
